TPU v7x, 128 devices: a whole 4x4x4 slice. The times are simulated.
128 devices in a mesh: dp: 8 (over z, core), fsdp: 16 (over x, y).
Axes of the slice: x: 4, y: 4, z: 4, core: 2. Of those that a mesh axis runs over, the one named last changes fastest.
Arguments:
- gate_act: bfloat16 [4096, 14848], P('fsdp', 'dp'), may hold values from -6 to 6
- up_act: bfloat16 [4096, 14848], P('fsdp', 'dp'), may hold values from -6 to 6
- out_grad: bfloat16 [4096, 4096], P('fsdp'), may hold values from -6 to 6
- master_old: float32 [8, 2176, 4096], P('dp', 'fsdp'), may hold values from -0.046875 to 0.046875
- moment1_old: float32 [8, 2176, 4096], P('dp', 'fsdp'), may hold values from -4 to 4
- moment2_old: float32 [8, 2176, 4096], P('dp', 'fsdp'), may hold values from 0.02 to 4
- old_bounds: int32 [8, 17], P('dp'), may hold values from 0 to 1856, as said below
- new_bounds: int32 [8, 16], P('dp'), may hold values from 0 to 1856, as said below
- rank_map: int32 [8, 16], P('dp'), may hold values from 0 to 15, as said below
Outputs:
- mlp_out: float32 [4096, 4096], P('fsdp', 'dp')
- master_new: float32 [8, 2176, 4096], P('dp', 'fsdp')
- moment1_new: float32 [8, 2176, 4096], P('dp', 'fsdp')
- moment2_new: float32 [8, 2176, 4096], P('dp', 'fsdp')
Inputs may be any that keep to these rules, and one draw needn't show every extreme that they name: Each row of old_bounds starts at 0, ends at 1856 and never falls; each position's rows fit its 136 slots. Each row of new_bounds starts at 0, ends at 1856 and never falls; each rank's rows fit 136 slots. In every block a position's new rows lie within its old rows and at most 58 rows of each of its two neighbours. `rank_map`: in each block's row exactly one position, one of the two middle ones, has rank 16 - 1 and owns nothing; the others hold the ranks 0 to 14 in position order.
All inputs are finite; a program needn't handle non-finite values.
Results may differ from a plain program's by a relative error of at most 0.012.
Values may be sent and summed in bfloat16 or wider, within the bound.
A program may use at most 192 MiB of HBM per device.

v0:
```python
import math
import jax
import jax.numpy as jnp
from jax import lax
from jax.sharding import PartitionSpec as P


def passed_along(value, axis, steps):
    count = lax.axis_size(axis)
    leading, last = (max(0, -steps), min(count, count - steps))
    return lax.ppermute(value, axis, [(source, source + steps) for source in range(leading, last)])


def pick_entry(table, index):
    return jnp.sum(jnp.where(jnp.arange(table.shape[0]) == index, table, jnp.zeros_like(table)))


def migrate(stacked, moved_rows, my_old_start, my_old_count, my_new_start, my_new_count):
    slot_rows = stacked.shape[1]
    prefix = stacked[:, :moved_rows]
    padded = jnp.concatenate(
        [jnp.zeros((3, moved_rows, stacked.shape[2]), stacked.dtype), stacked], axis=1
    )
    suffix = lax.dynamic_slice_in_dim(padded, my_old_count, moved_rows, 1)
    from_right = passed_along(prefix.astype(jnp.bfloat16), "fsdp", -1).astype(prefix.dtype)
    from_left = passed_along(suffix.astype(jnp.bfloat16), "fsdp", 1).astype(suffix.dtype)
    source = jnp.concatenate([from_left, stacked, from_right], axis=1)
    row_index = jnp.arange(slot_rows)
    global_row = my_new_start + row_index
    my_old_end = my_old_start + my_old_count
    index = (
        moved_rows
        + global_row
        - my_old_start
        + jnp.where(global_row >= my_old_end, slot_rows - my_old_count, 0)
    )
    index = jnp.clip(index, 0, 2 * moved_rows + slot_rows - 1)
    chosen = jnp.take(source, index, axis=1)
    return jnp.where((row_index < my_new_count)[None, :, None], chosen, jnp.zeros_like(chosen))


def block_product(hidden, weight_shard, table_start, table_count):
    slot_rows = weight_shard.shape[0]
    padded_hidden = jnp.concatenate(
        [hidden, jnp.zeros((hidden.shape[0], slot_rows), hidden.dtype)], axis=1
    )
    row_index = jnp.arange(slot_rows)[:, None]
    empty = jnp.zeros((hidden.shape[0], weight_shard.shape[1]), jnp.float32)
    piece = lax.all_gather(weight_shard, "fsdp", axis=0, tiled=True)
    shard_count = piece.shape[0] // slot_rows
    blocks = piece.reshape(shard_count, slot_rows, piece.shape[1])

    def one_shard(step, carry):
        start_col = pick_entry(table_start, step)
        live_rows = pick_entry(table_count, step)
        block = lax.dynamic_index_in_dim(blocks, step, 0, keepdims=False)
        block = jnp.where(row_index < live_rows, block, jnp.zeros_like(block))
        columns = lax.dynamic_slice_in_dim(padded_hidden, start_col, slot_rows, 1)
        return carry + jnp.dot(columns, block, preferred_element_type=jnp.float32)

    return lax.fori_loop(0, shard_count, one_shard, empty)


def local(
    gate_act,
    up_act,
    out_grad,
    master_old,
    moment1_old,
    moment2_old,
    old_bounds,
    new_bounds,
    rank_map,
):
    ranks_total = lax.axis_size("fsdp")
    my_position = lax.axis_index("fsdp")
    slot_rows = master_old.shape[1]
    token_rows = gate_act.shape[0]
    block_rows = gate_act.shape[1]
    base_rows = block_rows // ranks_total
    moved_rows = (base_rows + 1) // 2
    grad_scale = 1.0 / math.sqrt(token_rows * ranks_total)
    my_old_bounds = old_bounds[0]
    my_new_bounds = new_bounds[0]
    my_rank_map = rank_map[0]
    old_start = my_old_bounds[:-1]
    old_count = my_old_bounds[1:] - my_old_bounds[:-1]
    extended = jnp.concatenate([my_new_bounds, my_new_bounds[-1:]])
    extended_next = jnp.concatenate([extended[1:], extended[-1:]])
    owner_hit = my_rank_map[:, None] == jnp.arange(ranks_total + 1)[None, :]
    new_start = jnp.sum(jnp.where(owner_hit, extended[None, :], 0), axis=1)
    new_count = jnp.sum(jnp.where(owner_hit, extended_next[None, :], 0), axis=1) - new_start
    hidden = (jax.nn.silu(gate_act.astype(jnp.float32)) * up_act.astype(jnp.float32)).astype(
        jnp.bfloat16
    )
    stacked = jnp.stack([master_old[0], moment1_old[0], moment2_old[0]])
    moved = migrate(
        stacked,
        moved_rows,
        pick_entry(old_start, my_position),
        pick_entry(old_count, my_position),
        pick_entry(new_start, my_position),
        pick_entry(new_count, my_position),
    )
    weight_shard = moved[0].astype(jnp.bfloat16)
    block_part = block_product(hidden, weight_shard, new_start, new_count)
    mlp_out = lax.psum_scatter(
        block_part.astype(jnp.bfloat16), "dp", scatter_dimension=1, tiled=True
    ).astype(jnp.float32)
    row_index = jnp.arange(slot_rows * lax.axis_size("fsdp"))
    position = row_index // slot_rows
    within = row_index % slot_rows
    hit = position[:, None] == jnp.arange(ranks_total)[None, :]
    start_col = jnp.sum(jnp.where(hit, new_start[None, :], 0), axis=1)
    live_rows = jnp.sum(jnp.where(hit, new_count[None, :], 0), axis=1)
    column = jnp.clip(start_col + within, 0, block_rows - 1)
    chosen = jnp.take(hidden, column, axis=1)
    chosen = jnp.where((within < live_rows)[None, :], chosen, jnp.zeros_like(chosen))
    grad = (
        lax.psum_scatter(
            lax.dot_general(
                chosen, out_grad, (((0,), (0,)), ((), ())), preferred_element_type=jnp.float32
            ).astype(jnp.bfloat16),
            "fsdp",
            scatter_dimension=0,
            tiled=True,
        ).astype(jnp.float32)
        * grad_scale
    )
    first_next = 0.9 * moved[1] + 0.1 * grad
    second_next = 0.95 * moved[2] + 0.05 * grad * grad
    master_next = moved[0] - 0.001 * (first_next / (jnp.sqrt(second_next) + 1e-08) + 0.1 * moved[0])
    return (mlp_out, master_next[None], first_next[None], second_next[None])


def solution(mesh):
    placed = (
        P("fsdp", "dp"),
        P("fsdp", "dp"),
        P("fsdp", None),
        P("dp", "fsdp", None),
        P("dp", "fsdp", None),
        P("dp", "fsdp", None),
        P("dp", None),
        P("dp", None),
        P("dp", None),
    )
    return jax.shard_map(
        local,
        mesh=mesh,
        in_specs=placed,
        out_specs=(
            P("fsdp", "dp"),
            P("dp", "fsdp", None),
            P("dp", "fsdp", None),
            P("dp", "fsdp", None),
        ),
        check_vma=False,
    )
```

profile of v0, /device:TPU:0, one launch (start us, length us, event | category | flops | bytes accessed | tf_op | source)
XLA Modules:
  0.0 450.1 jit_solution(16102866951896543829)
XLA Ops:
  18.3 3.4 constant_dynamic-update-slice_fusion.1
  23.2 5.2 %fusion.10 = (bf16[3,58,4096]{2,1,0:T(8,128)(2,1)}, bf16[3,58,4096]{2,1,0:T(8,128)(2,1)}) fusion(s32[]{:T(128)S(6)} %select_n.170, f32[3,136,4096]{2,1,0:T(8,128)} %constant_dynamic-update-slice_fusion), kind=kLoop, calls=%fused_computation.23 | loop fusion | bytes 11108356 | tf_op jit(solution)/shard_map/convert_element_type | solution.py:26
  28.4 4.8 %collective-permute-start = (bf16[3,58,4096]{2,1,0:T(8,128)(2,1)}, bf16[3,58,4096]{2,1,0:T(8,128)(2,1)}, u32[]{:S(2)}, u32[]{:S(2)}) collective-permute-start(bf16[3,58,4096]{2,1,0:T(8,128)(2,1)} %get-tuple-element.207), channel_id=1, source_target_pairs={{0,1},{1,2},{2,3},{3,4},{4,5},{5,6},{6,7},{7,8},{8,9},{9,10},{10,1... | collective-permute-start | bytes 4276232 | tf_op jit(solution)/shard_map/ppermute | solution.py:11
  39.6 26.3 %collective-permute-done = bf16[3,58,4096]{2,1,0:T(8,128)(2,1)} collective-permute-done((bf16[3,58,4096]{2,1,0:T(8,128)(2,1)}, bf16[3,58,4096]{2,1,0:T(8,128)(2,1)}, u32[]{:S(2)}, u32[]{:S(2)}) %collective-permute-start) | collective-permute-done | bytes 1425440 | tf_op jit(solution)/shard_map/ppermute | solution.py:11
  67.9 3.4 collective-permute-done.1
  75.1 23.1 %copy.39 = f32[3,252,4096]{2,0,1:T(4,128)} copy(f32[3,252,4096]{2,1,0:T(8,128)S(1)} %pad_maximum_fusion) | data formatting | bytes 24772608 | tf_op jit(solution)/shard_map/concatenate | solution.py:27
  98.2 17.2 %gather_fusion = f32[136,3,4096]{2,1,0:T(4,128)} fusion(f32[3,252,4096]{2,0,1:T(4,128)} %copy.39, s32[1024]{0:T(1024)S(1)} %pad_clamp_fusion.1), kind=kCustom, calls=%fused_computation | custom fusion | bytes 13369888 | tf_op jit(solution)/shard_map/jit(_take)/gather | solution.py:38
  115.4 12.2 %select_bitcast_fusion = f32[3,136,4096]{2,0,1:T(4,128)} fusion(f32[136,3,4096]{2,1,0:T(4,128)} %gather_fusion, pred[136]{0:T(512)(128)(4,1)S(1)} %iota_compare_fusion.2, pred[136]{0:T(512)(128)(4,1)S(1)} %compare_and_fusion.1), kind=kLoop, calls=%fused_computation.19 | loop fusion | flops 3342336 | bytes 13369616 | tf_op jit(solution)/shard_map/jit(_where)/select_n | solution.py:39
  127.7 16.3 %slice_multiply_fusion = (f32[1,136,4096]{2,0,1:T(1,128)}, f32[1,136,4096]{2,0,1:T(1,128)S(1)}, f32[1,136,4096]{2,0,1:T(1,128)}) fusion(f32[3,136,4096]{2,0,1:T(4,128)} %select_bitcast_fusion), kind=kLoop, calls=%fused_computation.30 | loop fusion | flops 557056 | bytes 13369344 | tf_op jit(solution)/shard_map/mul | solution.py:131
  149.9 7.7 %gather_fusion.1 = bf16[2176,256]{1,0:T(8,128)(2,1)} fusion(bf16[256,1856]{0,1:T(8,128)(2,1)S(1)} %fusion.20, s32[3072]{0:T(1024)S(1)} %pad_clamp_fusion), kind=kCustom, calls=%fused_computation.1 | custom fusion | bytes 2236928 | tf_op jit(solution)/shard_map/jit(_take)/gather | solution.py:117
  157.6 10.2 %convolution_convert_fusion = bf16[2176,4096]{1,0:T(8,128)(2,1)} fusion(bf16[256,4096]{1,0:T(8,128)(2,1)S(1)} %copy-done, bf16[2176,256]{1,0:T(8,128)(2,1)} %gather_fusion.1, pred[2176]{0:T(1024)(128)(4,1)S(1)} %fusion.32, pred[2176]{0:T(1024)(128)(4,1)S(1)} %compare_and_fusion), kind=kOutput, calls=%fused_computation.16 | convolution fusion | flops 4573429760 | bytes 21041408 | tf_op jit(solution)/shard_map/dot_general | solution.py:121
  168.0 98.5 %all-gather.2.cloned.1.call-done = bf16[2176,4096]{1,0:T(8,128)(2,1)} async-done(((bf16[136,4096]{1,0:T(8,128)(2,1)}), bf16[2176,4096]{1,0:T(8,128)(2,1)}) %all-gather.2.cloned.1.call-update) | async-done | bytes 17825808 | tf_op jit(solution)/shard_map/all_gather | solution.py:49
  266.5 137.3 %while.14 = (s32[]{:T(128)}, f32[256,4096]{1,0:T(8,128)}, s32[16]{0:T(128)S(1)}, bf16[256,1992]{0,1:T(8,128)(2,1)S(1)}, s32[16]{0:T(128)S(1)}, /*index=5*/bf16[1...) while((s32[]{:T(128)}, f32[256,4096]{1,0:T(8,128)}, s32[16]{0:T(128)S(1)}, ...), condition=%wide.region_9.10_spmd.clone, body=%wide.region_6.9_spmd.clone.sunk | while | flops 287867104 | bytes 9573797 | solution.py:61
  269.7 4.0 convolution_add_fusion.2
  277.0 5.8 %convolution_add_fusion.2 = f32[256,4096]{1,0:T(8,128)} fusion(f32[256,4096]{1,0:T(8,128)} %get-tuple-element.267, pred[]{:T(512)S(6)} %compare.5, bf16[16,136,4096]{2,1,0:T(8,128)(2,1)} %get-tuple-element.280, s32[]{:T(128)} %get-tuple-element.266, pred[136]{0:T(512)(128)(4,1)S(1)} %compare_reduce_fusion.2, ...), kind=kOutput, calls=%fused_computation.3.clone.1 | convolution fusion | flops 287866880 | bytes 9573381 | tf_op jit(solution)/shard_map/while/body/eval_jaxpr/dot_general | solution.py:59
  286.1 5.4 %convolution_add_fusion.2 = f32[256,4096]{1,0:T(8,128)} fusion(f32[256,4096]{1,0:T(8,128)} %get-tuple-element.267, pred[]{:T(512)S(6)} %compare.5, bf16[16,136,4096]{2,1,0:T(8,128)(2,1)} %get-tuple-element.280, s32[]{:T(128)} %get-tuple-element.266, pred[136]{0:T(512)(128)(4,1)S(1)} %compare_reduce_fusion.2, ...), kind=kOutput, calls=%fused_computation.3.clone.1 | convolution fusion | flops 287866880 | bytes 9573381 | tf_op jit(solution)/shard_map/while/body/eval_jaxpr/dot_general | solution.py:59
  294.7 5.3 %convolution_add_fusion.2 = f32[256,4096]{1,0:T(8,128)} fusion(f32[256,4096]{1,0:T(8,128)} %get-tuple-element.267, pred[]{:T(512)S(6)} %compare.5, bf16[16,136,4096]{2,1,0:T(8,128)(2,1)} %get-tuple-element.280, s32[]{:T(128)} %get-tuple-element.266, pred[136]{0:T(512)(128)(4,1)S(1)} %compare_reduce_fusion.2, ...), kind=kOutput, calls=%fused_computation.3.clone.1 | convolution fusion | flops 287866880 | bytes 9573381 | tf_op jit(solution)/shard_map/while/body/eval_jaxpr/dot_general | solution.py:59
  303.3 5.5 %convolution_add_fusion.2 = f32[256,4096]{1,0:T(8,128)} fusion(f32[256,4096]{1,0:T(8,128)} %get-tuple-element.267, pred[]{:T(512)S(6)} %compare.5, bf16[16,136,4096]{2,1,0:T(8,128)(2,1)} %get-tuple-element.280, s32[]{:T(128)} %get-tuple-element.266, pred[136]{0:T(512)(128)(4,1)S(1)} %compare_reduce_fusion.2, ...), kind=kOutput, calls=%fused_computation.3.clone.1 | convolution fusion | flops 287866880 | bytes 9573381 | tf_op jit(solution)/shard_map/while/body/eval_jaxpr/dot_general | solution.py:59
  312.1 5.4 %convolution_add_fusion.2 = f32[256,4096]{1,0:T(8,128)} fusion(f32[256,4096]{1,0:T(8,128)} %get-tuple-element.267, pred[]{:T(512)S(6)} %compare.5, bf16[16,136,4096]{2,1,0:T(8,128)(2,1)} %get-tuple-element.280, s32[]{:T(128)} %get-tuple-element.266, pred[136]{0:T(512)(128)(4,1)S(1)} %compare_reduce_fusion.2, ...), kind=kOutput, calls=%fused_computation.3.clone.1 | convolution fusion | flops 287866880 | bytes 9573381 | tf_op jit(solution)/shard_map/while/body/eval_jaxpr/dot_general | solution.py:59
  320.7 5.4 %convolution_add_fusion.2 = f32[256,4096]{1,0:T(8,128)} fusion(f32[256,4096]{1,0:T(8,128)} %get-tuple-element.267, pred[]{:T(512)S(6)} %compare.5, bf16[16,136,4096]{2,1,0:T(8,128)(2,1)} %get-tuple-element.280, s32[]{:T(128)} %get-tuple-element.266, pred[136]{0:T(512)(128)(4,1)S(1)} %compare_reduce_fusion.2, ...), kind=kOutput, calls=%fused_computation.3.clone.1 | convolution fusion | flops 287866880 | bytes 9573381 | tf_op jit(solution)/shard_map/while/body/eval_jaxpr/dot_general | solution.py:59
  329.4 5.4 %convolution_add_fusion.2 = f32[256,4096]{1,0:T(8,128)} fusion(f32[256,4096]{1,0:T(8,128)} %get-tuple-element.267, pred[]{:T(512)S(6)} %compare.5, bf16[16,136,4096]{2,1,0:T(8,128)(2,1)} %get-tuple-element.280, s32[]{:T(128)} %get-tuple-element.266, pred[136]{0:T(512)(128)(4,1)S(1)} %compare_reduce_fusion.2, ...), kind=kOutput, calls=%fused_computation.3.clone.1 | convolution fusion | flops 287866880 | bytes 9573381 | tf_op jit(solution)/shard_map/while/body/eval_jaxpr/dot_general | solution.py:59
  338.1 5.4 %convolution_add_fusion.2 = f32[256,4096]{1,0:T(8,128)} fusion(f32[256,4096]{1,0:T(8,128)} %get-tuple-element.267, pred[]{:T(512)S(6)} %compare.5, bf16[16,136,4096]{2,1,0:T(8,128)(2,1)} %get-tuple-element.280, s32[]{:T(128)} %get-tuple-element.266, pred[136]{0:T(512)(128)(4,1)S(1)} %compare_reduce_fusion.2, ...), kind=kOutput, calls=%fused_computation.3.clone.1 | convolution fusion | flops 287866880 | bytes 9573381 | tf_op jit(solution)/shard_map/while/body/eval_jaxpr/dot_general | solution.py:59
  346.7 5.4 %convolution_add_fusion.2 = f32[256,4096]{1,0:T(8,128)} fusion(f32[256,4096]{1,0:T(8,128)} %get-tuple-element.267, pred[]{:T(512)S(6)} %compare.5, bf16[16,136,4096]{2,1,0:T(8,128)(2,1)} %get-tuple-element.280, s32[]{:T(128)} %get-tuple-element.266, pred[136]{0:T(512)(128)(4,1)S(1)} %compare_reduce_fusion.2, ...), kind=kOutput, calls=%fused_computation.3.clone.1 | convolution fusion | flops 287866880 | bytes 9573381 | tf_op jit(solution)/shard_map/while/body/eval_jaxpr/dot_general | solution.py:59
  355.4 5.3 %convolution_add_fusion.2 = f32[256,4096]{1,0:T(8,128)} fusion(f32[256,4096]{1,0:T(8,128)} %get-tuple-element.267, pred[]{:T(512)S(6)} %compare.5, bf16[16,136,4096]{2,1,0:T(8,128)(2,1)} %get-tuple-element.280, s32[]{:T(128)} %get-tuple-element.266, pred[136]{0:T(512)(128)(4,1)S(1)} %compare_reduce_fusion.2, ...), kind=kOutput, calls=%fused_computation.3.clone.1 | convolution fusion | flops 287866880 | bytes 9573381 | tf_op jit(solution)/shard_map/while/body/eval_jaxpr/dot_general | solution.py:59
  364.0 5.3 %convolution_add_fusion.2 = f32[256,4096]{1,0:T(8,128)} fusion(f32[256,4096]{1,0:T(8,128)} %get-tuple-element.267, pred[]{:T(512)S(6)} %compare.5, bf16[16,136,4096]{2,1,0:T(8,128)(2,1)} %get-tuple-element.280, s32[]{:T(128)} %get-tuple-element.266, pred[136]{0:T(512)(128)(4,1)S(1)} %compare_reduce_fusion.2, ...), kind=kOutput, calls=%fused_computation.3.clone.1 | convolution fusion | flops 287866880 | bytes 9573381 | tf_op jit(solution)/shard_map/while/body/eval_jaxpr/dot_general | solution.py:59
  372.6 5.4 %convolution_add_fusion.2 = f32[256,4096]{1,0:T(8,128)} fusion(f32[256,4096]{1,0:T(8,128)} %get-tuple-element.267, pred[]{:T(512)S(6)} %compare.5, bf16[16,136,4096]{2,1,0:T(8,128)(2,1)} %get-tuple-element.280, s32[]{:T(128)} %get-tuple-element.266, pred[136]{0:T(512)(128)(4,1)S(1)} %compare_reduce_fusion.2, ...), kind=kOutput, calls=%fused_computation.3.clone.1 | convolution fusion | flops 287866880 | bytes 9573381 | tf_op jit(solution)/shard_map/while/body/eval_jaxpr/dot_general | solution.py:59
  381.2 5.4 %convolution_add_fusion.2 = f32[256,4096]{1,0:T(8,128)} fusion(f32[256,4096]{1,0:T(8,128)} %get-tuple-element.267, pred[]{:T(512)S(6)} %compare.5, bf16[16,136,4096]{2,1,0:T(8,128)(2,1)} %get-tuple-element.280, s32[]{:T(128)} %get-tuple-element.266, pred[136]{0:T(512)(128)(4,1)S(1)} %compare_reduce_fusion.2, ...), kind=kOutput, calls=%fused_computation.3.clone.1 | convolution fusion | flops 287866880 | bytes 9573381 | tf_op jit(solution)/shard_map/while/body/eval_jaxpr/dot_general | solution.py:59
  389.9 5.3 %convolution_add_fusion.2 = f32[256,4096]{1,0:T(8,128)} fusion(f32[256,4096]{1,0:T(8,128)} %get-tuple-element.267, pred[]{:T(512)S(6)} %compare.5, bf16[16,136,4096]{2,1,0:T(8,128)(2,1)} %get-tuple-element.280, s32[]{:T(128)} %get-tuple-element.266, pred[136]{0:T(512)(128)(4,1)S(1)} %compare_reduce_fusion.2, ...), kind=kOutput, calls=%fused_computation.3.clone.1 | convolution fusion | flops 287866880 | bytes 9573381 | tf_op jit(solution)/shard_map/while/body/eval_jaxpr/dot_general | solution.py:59
  398.5 5.3 %convolution_add_fusion.2 = f32[256,4096]{1,0:T(8,128)} fusion(f32[256,4096]{1,0:T(8,128)} %get-tuple-element.267, pred[]{:T(512)S(6)} %compare.5, bf16[16,136,4096]{2,1,0:T(8,128)(2,1)} %get-tuple-element.280, s32[]{:T(128)} %get-tuple-element.266, pred[136]{0:T(512)(128)(4,1)S(1)} %compare_reduce_fusion.2, ...), kind=kOutput, calls=%fused_computation.3.clone.1 | convolution fusion | flops 287866880 | bytes 9573381 | tf_op jit(solution)/shard_map/while/body/eval_jaxpr/dot_general | solution.py:59
  403.8 3.8 convert_element_type.41
  407.7 12.8 %fusion.24 = (f32[1,136,4096]{2,1,0:T(8,128)}, f32[1,136,4096]{2,1,0:T(8,128)}, f32[1,136,4096]{2,1,0:T(8,128)}) fusion(bf16[136,4096]{1,0:T(8,128)(2,1)} %reduce-scatter.7.cloned.1.call-done, f32[1,136,4096]{2,0,1:T(1,128)} %get-tuple-element.204, f32[1,136,4096]{2,0,1:T(1,128)} %get-tuple-element.206, f32[1,136,4096]{2,0,1:T(1,128)} %copy-done.3), kind=kLoop, calls=%fused_computation.44 | loop fusion | flops 7798784 | bytes 14483456 | tf_op jit(solution)/shard_map/broadcast_in_dim | solution.py:133
  420.5 21.3 %reduce-scatter.5.cloned.1.call-done = bf16[256,512]{1,0:T(8,128)(2,1)} async-done(((bf16[256,4096]{1,0:T(8,128)(2,1)}), bf16[256,512]{1,0:T(8,128)(2,1)}) %reduce-scatter.5.cloned.1.call-update) | async-done | bytes 262160 | tf_op jit(solution)/shard_map/reduce_scatter | solution.py:107
  (76 shorter events, 49.6 us)
Async XLA Ops:
  7.2 150.4 %copy-start = (bf16[256,4096]{1,0:T(8,128)(2,1)S(1)}, bf16[256,4096]{1,0:T(8,128)(2,1)}, u32[]{:S(2)}) copy-start(bf16[256,4096]{1,0:T(8,128)(2,1)} %param.13) | copy-start | bytes 6291460
  7.2 259.3 %all-gather.2.cloned.1.call-start = ((), (), s32[]{:S(2)}) async-start(), calls=%async_computation.2 | async-start | bytes 18939904 | tf_op jit(solution)/shard_map/all_gather | solution.py:49
  18.3 3.4 copy-start.4
  28.4 37.5 %collective-permute-start = (bf16[3,58,4096]{2,1,0:T(8,128)(2,1)}, bf16[3,58,4096]{2,1,0:T(8,128)(2,1)}, u32[]{:S(2)}, u32[]{:S(2)}) collective-permute-start(bf16[3,58,4096]{2,1,0:T(8,128)(2,1)} %get-tuple-element.207), channel_id=1, source_target_pairs={{0,1},{1,2},{2,3},{3,4},{4,5},{5,6},{6,7},{7,8},{8,9},{9,10},{10,1... | collective-permute-start | bytes 4276232 | tf_op jit(solution)/shard_map/ppermute | solution.py:11
  33.2 38.1 %collective-permute-start.1 = (bf16[3,58,4096]{2,1,0:T(8,128)(2,1)}, bf16[3,58,4096]{2,1,0:T(8,128)(2,1)}, u32[]{:S(2)}, u32[]{:S(2)}) collective-permute-start(bf16[3,58,4096]{2,1,0:T(8,128)(2,1)} %get-tuple-element.208), channel_id=1, source_target_pairs={{1,0},{2,1},{3,2},{4,3},{5,4},{6,5},{7,6},{8,7},{9,8},{10,9},{11,1... | collective-permute-start | bytes 4276232 | tf_op jit(solution)/shard_map/ppermute | solution.py:11
  65.9 7.1 %copy-start.2 = (f32[3,136,4096]{2,1,0:T(8,128)S(1)}, f32[3,136,4096]{2,1,0:T(8,128)}, u32[]{:S(2)}) copy-start(f32[3,136,4096]{2,1,0:T(8,128)} %constant_dynamic-update-slice_fusion) | copy-start | bytes 20054020
  143.9 1.4 copy-start.3
  147.5 260.1 %reduce-scatter.7.cloned.1.call-start = ((), (), s32[]{:S(2)}) async-start(), calls=%async_computation.4 | async-start | bytes 18939904
  167.9 273.9 %reduce-scatter.5.cloned.1.call-start = ((), (), s32[]{:S(2)}) async-start(), calls=%async_computation.3 | async-start | bytes 2359296 | tf_op jit(solution)/shard_map/reduce_scatter | solution.py:107
  407.6 35.9 %copy-start.1 = (bf16[256,4096]{1,0:T(8,128)(2,1)S(1)}, bf16[256,4096]{1,0:T(8,128)(2,1)}, u32[]{:S(2)}) copy-start(bf16[256,4096]{1,0:T(8,128)(2,1)} %param.13) | copy-start | bytes 6291460
Sparse Core Ops, SparseCore 0:
  147.6 118.7 all-gather.1
  269.9 115.5 reduce-scatter.6
  407.7 34.0 reduce-scatter.4
where the time goes:
time: 451 us; the launch traced here: 450 us
  waiting for transfers between devices  150 us (33%)
  matrix products  95.4 us (21%)
  other arithmetic  83.4 us (18%)
  local copies, waits for them, and re-layouts  66.4 us (15%)
  loops' own time  31.3 us (7%)
  between operations  17.8 us (4%)
  starting transfers between devices  6.23 us (1%)
    all_gather x1, waiting for transfers between devices, block_product(): piece = lax.all_gather(weight_shard, 'fsdp', axis=0, tiled=True)  98.5 us
    dot_general x16, matrix products, one_shard(): return carry + jnp.dot(columns, block, preferred_element_type=jnp.float32)  85.1 us
    another operation x1, loops' own time, block_product(): return lax.fori_loop(0, shard_count, one_shard, empty)  31.3 us
    ppermute x2, waiting for transfers between devices, passed_along(): lax.ppermute(value, axis, [(source, source + steps) for source in range(l...  29.8 us
    concatenate x1, local copies, waits for them, and re-layouts, migrate(): source = jnp.concatenate([from_left, stacked, from_right], axis=1)  23.1 us
    reduce_scatter x1, waiting for transfers between devices, local(): lax.psum_scatter(block_part.astype(jnp.bfloat16), 'dp', scatter_dimension...  21.3 us
    gather x1, local copies, waits for them, and re-layouts, migrate(): chosen = jnp.take(source, index, axis=1)  17.2 us
    mul x1, other arithmetic, local(): second_next = 0.95 * moved[2] + 0.05 * grad * grad  16.3 us
  transfers between devices with their start and end apart: 5, of which 4 were waited for; matrix products, arithmetic and copies ran while one was open for 33% of the time, Pallas kernels for 0%

commit v1 on v0

--- a/solution.py
+++ b/solution.py
@@ -3,6 +3,13 @@
 import jax.numpy as jnp
 from jax import lax
 from jax.sharding import PartitionSpec as P
+
+
+def all_by_exchange(x, axis, dim):
+    devices = lax.axis_size(axis)
+    pieces = jnp.stack([x for _ in range(devices)])
+    pieces = lax.all_to_all(pieces, axis, split_axis=0, concat_axis=0)
+    return jnp.concatenate(pieces, axis=dim)
 
 
 def passed_along(value, axis, steps):
@@ -46,7 +53,7 @@
     )
     row_index = jnp.arange(slot_rows)[:, None]
     empty = jnp.zeros((hidden.shape[0], weight_shard.shape[1]), jnp.float32)
-    piece = lax.all_gather(weight_shard, "fsdp", axis=0, tiled=True)
+    piece = all_by_exchange(weight_shard, "fsdp", 0)
     shard_count = piece.shape[0] // slot_rows
     blocks = piece.reshape(shard_count, slot_rows, piece.shape[1])
 

time: 451 us -> 794 us (1.76)
  waiting for transfers between devices: 150 us -> 479 us
    all_to_all x0 -> x1, waiting for transfers between devices: none -> 311 us  [all_by_exchange(): pieces = lax.all_to_all(pieces, axis, split_axis=0, concat_axis=0)]
    unnamed x4 -> x3, waiting for transfers between devices: 0.07 us -> 116 us
    all_gather x1 -> x0, waiting for transfers between devices: 98.5 us -> none  [block_product(): piece = lax.all_gather(weight_shard, 'fsdp', axis=0, tiled=True)]
  transfers between devices with their start and end apart: 5 -> 5, of which waited for: 4 -> 5; matrix products, arithmetic and copies ran while one was open for 33% -> 4% of each run, Pallas kernels for 0% -> 0%
where the time goes in v1:
time: 794 us; the launch traced here: 792 us
  waiting for transfers between devices  479 us (60%)
  matrix products  94.1 us (12%)
  other arithmetic  83.2 us (10%)
  local copies, waits for them, and re-layouts  72.7 us (9%)
  loops' own time  31.2 us (4%)
  between operations  18.1 us (2%)
  starting transfers between devices  13.3 us (2%)
    all_to_all x1, waiting for transfers between devices, all_by_exchange(): pieces = lax.all_to_all(pieces, axis, split_axis=0, concat_axis=0)  311 us
    unnamed x3, waiting for transfers between devices  116 us
    dot_general x16, matrix products, one_shard(): return carry + jnp.dot(columns, block, preferred_element_type=jnp.float32)  83.8 us
    another operation x1, loops' own time, block_product(): return lax.fori_loop(0, shard_count, one_shard, empty)  31.2 us
    ppermute x2, waiting for transfers between devices, passed_along(): lax.ppermute(value, axis, [(source, source + steps) for source in range(l...  29.8 us
    concatenate x1, local copies, waits for them, and re-layouts, migrate(): source = jnp.concatenate([from_left, stacked, from_right], axis=1)  23.1 us
    reduce_scatter x1, waiting for transfers between devices, local(): lax.psum_scatter(block_part.astype(jnp.bfloat16), 'dp', scatter_dimension...  22.3 us
    gather x1, local copies, waits for them, and re-layouts, migrate(): chosen = jnp.take(source, index, axis=1)  17.2 us
  transfers between devices with their start and end apart: 5, of which 5 were waited for; matrix products, arithmetic and copies ran while one was open for 4% of the time, Pallas kernels for 0%

profile of v1, /device:TPU:0, one launch (start us, length us, event | category | flops | bytes accessed | tf_op | source)
XLA Modules:
  0.0 792.1 jit_solution(5252869814034566214)
XLA Ops:
  23.2 5.2 fusion.10
  28.4 4.8 collective-permute-start
  39.6 26.3 %collective-permute-done = bf16[3,58,4096]{2,1,0:T(8,128)(2,1)} collective-permute-done((bf16[3,58,4096]{2,1,0:T(8,128)(2,1)}, bf16[3,58,4096]{2,1,0:T(8,128)(2,1)}, u32[]{:S(2)}, u32[]{:S(2)}) %collective-permute-start) | collective-permute-done | bytes 1425440 | tf_op jit(solution)/shard_map/ppermute | solution.py:18
  75.1 23.1 %copy.39 = f32[3,252,4096]{2,0,1:T(4,128)} copy(f32[3,252,4096]{2,1,0:T(8,128)S(1)} %pad_maximum_fusion) | data formatting | bytes 24772608 | tf_op jit(solution)/shard_map/concatenate | solution.py:34
  98.2 17.2 %gather_fusion = f32[136,3,4096]{2,1,0:T(4,128)} fusion(f32[3,252,4096]{2,0,1:T(4,128)} %copy.39, s32[1024]{0:T(1024)S(1)} %pad_clamp_fusion.1), kind=kCustom, calls=%fused_computation | custom fusion | bytes 13369888 | tf_op jit(solution)/shard_map/jit(_take)/gather | solution.py:45
  115.4 12.2 %select_bitcast_fusion = f32[3,136,4096]{2,0,1:T(4,128)} fusion(f32[136,3,4096]{2,1,0:T(4,128)} %gather_fusion, pred[136]{0:T(512)(128)(4,1)S(1)} %iota_compare_fusion.2, pred[136]{0:T(512)(128)(4,1)S(1)} %compare_and_fusion.1), kind=kLoop, calls=%fused_computation.19 | loop fusion | flops 3342336 | bytes 13369616 | tf_op jit(solution)/shard_map/jit(_where)/select_n | solution.py:46
  127.6 16.3 %slice_multiply_fusion = (f32[1,136,4096]{2,0,1:T(1,128)}, f32[1,136,4096]{2,0,1:T(1,128)S(1)}, f32[1,136,4096]{2,0,1:T(1,128)}) fusion(f32[3,136,4096]{2,0,1:T(4,128)} %select_bitcast_fusion), kind=kLoop, calls=%fused_computation.30 | loop fusion | flops 557056 | bytes 13369344 | tf_op jit(solution)/shard_map/mul | solution.py:138
  146.5 6.4 stack.8
  152.8 7.1 all-to-all-start
  163.1 311.2 %all-to-all-done = bf16[16,136,4096]{2,1,0:T(8,128)(2,1)} async-done(((bf16[16,136,4096]{2,1,0:T(8,128)(2,1)}), bf16[16,136,4096]{2,1,0:T(8,128)(2,1)}, u32[]{:S(2)}, u32[]{:S(2)}) %all-to-all-start) | async-done | bytes 17825824 | tf_op jit(solution)/shard_map/all_to_all | solution.py:11
  474.2 135.9 %while.14 = (s32[]{:T(128)}, f32[256,4096]{1,0:T(8,128)}, s32[16]{0:T(128)S(1)}, bf16[256,1992]{0,1:T(8,128)(2,1)}, s32[16]{0:T(128)S(1)}, /*index=5*/bf16[16,13...) while((s32[]{:T(128)}, f32[256,4096]{1,0:T(8,128)}, s32[16]{0:T(128)S(1)}, ...), condition=%wide.region_9.10_spmd.clone, body=%wide.region_6.9_spmd.clone.sunk | while | flops 287867104 | bytes 9573421 | solution.py:68
  477.5 4.0 convolution_add_fusion.2
  484.8 5.3 convolution_add_fusion.2
  493.4 5.3 convolution_add_fusion.2
  501.9 5.3 convolution_add_fusion.2
  510.5 5.3 convolution_add_fusion.2
  519.1 5.3 convolution_add_fusion.2
  527.7 5.3 convolution_add_fusion.2
  536.2 5.3 convolution_add_fusion.2
  544.8 5.3 convolution_add_fusion.2
  553.4 5.3 convolution_add_fusion.2
  561.9 5.3 convolution_add_fusion.2
  570.5 5.3 convolution_add_fusion.2
  579.1 5.3 convolution_add_fusion.2
  587.7 5.3 convolution_add_fusion.2
  596.2 5.3 convolution_add_fusion.2
  604.8 5.3 convolution_add_fusion.2
  614.2 7.7 gather_fusion.1
  622.0 10.3 %convolution_convert_fusion = bf16[2176,4096]{1,0:T(8,128)(2,1)} fusion(bf16[256,4096]{1,0:T(8,128)(2,1)S(1)} %copy-done, bf16[2176,256]{1,0:T(8,128)(2,1)} %gather_fusion.1, pred[2176]{0:T(1024)(128)(4,1)S(1)} %fusion.35, pred[2176]{0:T(1024)(128)(4,1)S(1)} %compare_and_fusion), kind=kOutput, calls=%fused_computation.16 | convolution fusion | flops 4573429760 | bytes 21041408 | tf_op jit(solution)/shard_map/dot_general | solution.py:128
  632.3 22.3 %reduce-scatter.5.cloned.1.call-done = bf16[256,512]{1,0:T(8,128)(2,1)} async-done(((bf16[256,4096]{1,0:T(8,128)(2,1)}), bf16[256,512]{1,0:T(8,128)(2,1)}) %reduce-scatter.5.cloned.1.call-update) | async-done | bytes 262160 | tf_op jit(solution)/shard_map/reduce_scatter | solution.py:114
  656.4 116.1 %reduce-scatter.7.cloned.1.call-done = bf16[136,4096]{1,0:T(8,128)(2,1)} async-done(((bf16[2176,4096]{1,0:T(8,128)(2,1)}), bf16[136,4096]{1,0:T(8,128)(2,1)}) %reduce-scatter.7.cloned.1.call-update) | async-done | bytes 1114128
  772.5 12.7 %fusion.27 = (f32[1,136,4096]{2,1,0:T(8,128)}, f32[1,136,4096]{2,1,0:T(8,128)}, f32[1,136,4096]{2,1,0:T(8,128)}) fusion(bf16[136,4096]{1,0:T(8,128)(2,1)} %reduce-scatter.7.cloned.1.call-done, f32[1,136,4096]{2,0,1:T(1,128)} %get-tuple-element.204, f32[1,136,4096]{2,0,1:T(1,128)} %get-tuple-element.206, f32[1,136,4096]{2,0,1:T(1,128)} %copy-done.2), kind=kLoop, calls=%fused_computation.48 | loop fusion | flops 7798784 | bytes 14483456 | tf_op jit(solution)/shard_map/broadcast_in_dim | solution.py:140
  (74 shorter events, 60.0 us)
Async XLA Ops:
  7.2 614.8 %copy-start = (bf16[256,4096]{1,0:T(8,128)(2,1)S(1)}, bf16[256,4096]{1,0:T(8,128)(2,1)}, u32[]{:S(2)}) copy-start(bf16[256,4096]{1,0:T(8,128)(2,1)} %param.13) | copy-start | bytes 6291460
  18.3 3.4 copy-start.3
  28.4 37.5 %collective-permute-start = (bf16[3,58,4096]{2,1,0:T(8,128)(2,1)}, bf16[3,58,4096]{2,1,0:T(8,128)(2,1)}, u32[]{:S(2)}, u32[]{:S(2)}) collective-permute-start(bf16[3,58,4096]{2,1,0:T(8,128)(2,1)} %get-tuple-element.207), channel_id=1, source_target_pairs={{0,1},{1,2},{2,3},{3,4},{4,5},{5,6},{6,7},{7,8},{8,9},{9,10},{10,1... | collective-permute-start | bytes 4276232 | tf_op jit(solution)/shard_map/ppermute | solution.py:18
  33.2 38.1 %collective-permute-start.1 = (bf16[3,58,4096]{2,1,0:T(8,128)(2,1)}, bf16[3,58,4096]{2,1,0:T(8,128)(2,1)}, u32[]{:S(2)}, u32[]{:S(2)}) collective-permute-start(bf16[3,58,4096]{2,1,0:T(8,128)(2,1)} %get-tuple-element.208), channel_id=1, source_target_pairs={{1,0},{2,1},{3,2},{4,3},{5,4},{6,5},{7,6},{8,7},{9,8},{10,9},{11,1... | collective-permute-start | bytes 4276232 | tf_op jit(solution)/shard_map/ppermute | solution.py:18
  65.9 7.1 copy-start.1
  143.9 1.4 copy-start.2
  152.8 321.4 %all-to-all-start = ((bf16[16,136,4096]{2,1,0:T(8,128)(2,1)}), bf16[16,136,4096]{2,1,0:T(8,128)(2,1)}, u32[]{:S(2)}, u32[]{:S(2)}) async-start(bf16[16,136,4096]{2,1,0:T(8,128)(2,1)} %stack.8), calls=%async_computation | async-start | bytes 35651584 | tf_op jit(solution)/shard_map/all_to_all | solution.py:11
  159.9 494.7 %reduce-scatter.5.cloned.1.call-start = ((), (), s32[]{:S(2)}) async-start(), calls=%async_computation.3 | async-start | bytes 2359296 | tf_op jit(solution)/shard_map/reduce_scatter | solution.py:114
  613.9 158.6 %reduce-scatter.7.cloned.1.call-start = ((), (), s32[]{:S(2)}) async-start(), calls=%async_computation.4 | async-start | bytes 18939904
Sparse Core Ops, SparseCore 0:
  614.1 40.4 reduce-scatter.4
  658.1 114.4 reduce-scatter.6
